TPU v7x, 256 devices: a whole 4x4x8 slice. The times are simulated.
256 devices in a mesh: dp: 32 (over z, y_hi, core), expert: 8 (over x, y_lo).
Axes of the slice: x: 4, y: 4 (y_hi: 2, y_lo: 2; y = y_hi * 2 + y_lo), z: 8, core: 2. Of those that a mesh axis runs over, the one named last changes fastest.
Arguments:
- tokens: bfloat16 [32768, 2048], P(('dp', 'expert')), may hold values from -24 to 24
- cotangent: bfloat16 [32768, 2048], P(('dp', 'expert')), may hold values from -24 to 24
- expert_ids: int32 [32768, 2], P(('dp', 'expert')), may hold values from 0 to 7, all different within a row; in each aligned block of 128 rows (0 to 127, 128 to 255, ...) at most 40 rows name the same one
- gate_weights: float32 [32768, 2], P(('dp', 'expert')), may hold values from 0.1 to 1
- partner: int32 [8], replicated, may hold values from 0 to 7, as said below
- w_gate: bfloat16 [8, 2048, 768], P('expert'), may hold values from -0.125 to 0.125
- w_up: bfloat16 [8, 2048, 768], P('expert'), may hold values from -0.125 to 0.125
- w_down: bfloat16 [8, 768, 2048], P('expert'), may hold values from -0.21875 to 0.21875
Outputs:
- mixed_out: bfloat16 [32768, 2048], P(('dp', 'expert'))
- token_grad: bfloat16 [32768, 2048], P(('dp', 'expert'))
- gate_grad: float32 [32768, 2], P(('dp', 'expert'))
- slot_grad_gate: float32 [8, 2048, 768], P('expert', 'dp')
- slot_grad_up: float32 [8, 2048, 768], P('expert', 'dp')
- slot_grad_down: float32 [8, 768, 2048], P('expert', None, 'dp')
Inputs may be any that keep to these rules, and one draw needn't show every extreme that they name: `expert_ids`: each row names 2 different experts. Among the 128 rows of one device no expert is named by more than 40 rows, and in every draw some device names some expert exactly 40 times. partner[partner[i]] = i and partner[i] != i for every slot i.
All inputs are finite; a program needn't handle non-finite values.
Results may differ from a plain program's by a relative error of at most 0.015.
Values may be sent and summed in bfloat16 or wider, within the bound.
A program may use at most 128 MiB of HBM per device.

v0:
```python
import jax
import jax.numpy as jnp
from jax import lax
from jax.sharding import PartitionSpec as P


def as_sent(shard):

    def short(part):
        return part.astype(jnp.bfloat16) if part.dtype == jnp.float32 else part

    return jax.tree.map(short, shard)


def contract_rows(left_mat, right_mat):
    return lax.dot_general(
        left_mat, right_mat, (((0,), (0,)), ((), ())), preferred_element_type=jnp.float32
    )


def contract_cols(left_mat, right_mat):
    return lax.dot_general(
        left_mat, right_mat, (((1,), (1,)), ((), ())), preferred_element_type=jnp.float32
    )


def pick_from(stacked, source):
    return lax.dynamic_index_in_dim(stacked, source, 0, keepdims=False)


def shards(tokens, cotangent, expert_ids, gate_weights, partner, w_gate, w_up, w_down):
    groups = lax.axis_size("expert")
    my_group = lax.axis_index("expert")
    tok_count, model_width = tokens.shape
    top_count = expert_ids.shape[1]
    capacity = min(tok_count, 5 * tok_count * top_count // (4 * groups))
    buffer_rows = groups * capacity
    group_ids = jnp.arange(groups, dtype=jnp.int32)
    my_mate = pick_from(partner, my_group)
    flat_ids = expert_ids.reshape(-1)
    dest_group = jnp.sum(
        jnp.where(flat_ids[:, None] == group_ids[None, :], partner[None, :], 0), axis=1
    )
    one_hot = (dest_group[:, None] == group_ids[None, :]).astype(jnp.int32)
    earlier = jnp.cumsum(one_hot, axis=0) - one_hot
    slot_index = dest_group * capacity + jnp.sum(earlier * one_hot, axis=1)
    place_mat = (slot_index[None, :] == jnp.arange(buffer_rows, dtype=jnp.int32)[:, None]).astype(
        jnp.bfloat16
    )
    replicas = lax.axis_size("dp")
    share_rows = model_width // replicas
    share_start = lax.axis_index("dp") * share_rows
    shares = (
        lax.dynamic_slice_in_dim(w_gate[0], share_start, share_rows, 0),
        lax.dynamic_slice_in_dim(w_up[0], share_start, share_rows, 0),
        lax.dynamic_slice_in_dim(w_down[0], share_start, share_rows, 1),
    )
    is_mate = (partner == my_group)[:, None, None]
    outgoing = tuple(
        (
            jnp.where(is_mate, own_share[None], jnp.zeros_like(own_share)[None])
            for own_share in shares
        )
    )
    incoming = jax.tree.map(
        lambda part, own: part.astype(own.dtype),
        lax.all_to_all(as_sent(outgoing), "expert", split_axis=0, concat_axis=0, tiled=True),
        outgoing,
    )
    mate_shares = tuple((pick_from(block_piece, my_mate) for block_piece in incoming))
    gate_mat, up_mat, down_mat = (
        lax.all_gather(mate_shares[0], "dp", axis=0, tiled=True),
        lax.all_gather(mate_shares[1], "dp", axis=0, tiled=True),
        lax.all_gather(mate_shares[2], "dp", axis=1, tiled=True),
    )
    repeated = jnp.repeat(tokens, top_count, axis=0)
    outgoing_rows = jnp.dot(place_mat, repeated, preferred_element_type=jnp.float32).astype(
        jnp.bfloat16
    )
    expert_in = lax.all_to_all(
        outgoing_rows.reshape(groups, capacity, model_width),
        "expert",
        split_axis=0,
        concat_axis=0,
        tiled=True,
    ).reshape(buffer_rows, model_width)
    gate_pre = jnp.dot(expert_in, gate_mat, preferred_element_type=jnp.float32)
    up_pre = jnp.dot(expert_in, up_mat, preferred_element_type=jnp.float32)
    sigmoid_gate = jax.nn.sigmoid(gate_pre)
    hidden = (gate_pre * sigmoid_gate * up_pre).astype(jnp.bfloat16)
    expert_out = jnp.dot(hidden, down_mat, preferred_element_type=jnp.float32).astype(jnp.bfloat16)
    returned = lax.all_to_all(
        expert_out.reshape(groups, capacity, model_width),
        "expert",
        split_axis=0,
        concat_axis=0,
        tiled=True,
    ).reshape(buffer_rows, model_width)
    per_assign = (
        jnp.take(returned, slot_index, axis=0)
        .astype(jnp.float32)
        .reshape(tok_count, top_count, model_width)
    )
    mixed_out = jnp.sum(gate_weights[:, :, None] * per_assign, axis=1).astype(jnp.bfloat16)
    cot_float = cotangent.astype(jnp.float32)
    gate_grad = jnp.sum(cot_float[:, None, :] * per_assign, axis=2)
    scaled = (
        (gate_weights[:, :, None] * cot_float[:, None, :])
        .astype(jnp.bfloat16)
        .reshape(-1, model_width)
    )
    outgoing_grads = jnp.dot(place_mat, scaled, preferred_element_type=jnp.float32).astype(
        jnp.bfloat16
    )
    grads_in = lax.all_to_all(
        outgoing_grads.reshape(groups, capacity, model_width),
        "expert",
        split_axis=0,
        concat_axis=0,
        tiled=True,
    ).reshape(buffer_rows, model_width)
    hidden_grad = contract_cols(grads_in, down_mat)
    gate_grad_pre = (
        hidden_grad * up_pre * sigmoid_gate * (1.0 + gate_pre * (1.0 - sigmoid_gate))
    ).astype(jnp.bfloat16)
    up_grad_pre = (hidden_grad * gate_pre * sigmoid_gate).astype(jnp.bfloat16)
    row_grad = (contract_cols(gate_grad_pre, gate_mat) + contract_cols(up_grad_pre, up_mat)).astype(
        jnp.bfloat16
    )
    returned_grads = lax.all_to_all(
        row_grad.reshape(groups, capacity, model_width),
        "expert",
        split_axis=0,
        concat_axis=0,
        tiled=True,
    ).reshape(buffer_rows, model_width)
    grad_rows = (
        jnp.take(returned_grads, slot_index, axis=0)
        .astype(jnp.float32)
        .reshape(tok_count, top_count, model_width)
    )
    token_grad = jnp.sum(grad_rows, axis=1).astype(jnp.bfloat16)
    partial_gate = contract_rows(expert_in, gate_grad_pre)
    partial_up = contract_rows(expert_in, up_grad_pre)
    partial_down = contract_rows(hidden, grads_in)
    sum_gate, sum_up, sum_down = (
        lax.psum_scatter(
            partial_gate.astype(jnp.bfloat16), "dp", scatter_dimension=0, tiled=True
        ).astype(jnp.float32),
        lax.psum_scatter(
            partial_up.astype(jnp.bfloat16), "dp", scatter_dimension=0, tiled=True
        ).astype(jnp.float32),
        lax.psum_scatter(
            partial_down.astype(jnp.bfloat16), "dp", scatter_dimension=1, tiled=True
        ).astype(jnp.float32),
    )
    return (mixed_out, token_grad, gate_grad, sum_gate[None], sum_up[None], sum_down[None])


def solution(mesh):
    in_specs = (
        P(("dp", "expert"), None),
        P(("dp", "expert"), None),
        P(("dp", "expert"), None),
        P(("dp", "expert"), None),
        P(),
        P("expert", None, None),
        P("expert", None, None),
        P("expert", None, None),
    )
    out_specs = (
        P(("dp", "expert"), None),
        P(("dp", "expert"), None),
        P(("dp", "expert"), None),
        P("expert", "dp", None),
        P("expert", "dp", None),
        P("expert", None, "dp"),
    )
    return jax.shard_map(shards, mesh=mesh, in_specs=in_specs, out_specs=out_specs, check_vma=False)
```

profile of v0, /device:TPU:8, one launch (start us, length us, event | category | flops | bytes accessed | tf_op | source)
XLA Modules:
  0.0 687.3 jit_solution(8233593337685913203)
XLA Ops:
  7.2 0.8 broadcast_compare_fusion
  8.0 1.1 dynamic-slice_bitcast_fusion
  9.1 1.3 broadcast_select_fusion.3
  10.5 6.2 all-to-all-start.2
  19.2 8.9 %all-to-all-done.2 = bf16[8,64,768]{2,1,0:T(8,128)(2,1)} async-done(((bf16[8,64,768]{2,1,0:T(8,128)(2,1)}), bf16[8,64,768]{2,1,0:T(8,128)(2,1)}, u32[]{:S(2)}, u32[]{:S(2)}) %all-to-all-start.2) | async-done | bytes 786464 | tf_op jit(solution)/shard_map/all_to_all | solution.py:67
  28.1 1.5 constant_dynamic-slice_fusion.2
  30.1 15.1 %all_to_all.35 = bf16[8,768,64]{1,2,0:T(8,128)(2,1)S(1)} all-to-all(bf16[8,768,64]{1,2,0:T(8,128)(2,1)S(1)} %broadcast_select_fusion.1), channel_id=1, replica_groups=mesh['dp'=32,'expert'=8] {'expert'}, dimensions={0} | all-to-all | bytes 1572864 | tf_op jit(solution)/shard_map/all_to_all | solution.py:67
  45.2 0.6 constant_dynamic-slice_fusion
  46.0 13.8 %all_to_all.36 = bf16[8,64,768]{2,1,0:T(8,128)(2,1)S(1)} all-to-all(bf16[8,64,768]{2,1,0:T(8,128)(2,1)S(1)} %copy-done.6), channel_id=1, replica_groups=mesh['dp'=32,'expert'=8] {'expert'}, dimensions={0} | all-to-all | bytes 1572864 | tf_op jit(solution)/shard_map/all_to_all | solution.py:67
  59.8 0.6 constant_dynamic-slice_fusion.3
  62.9 1.6 convolution_convert_fusion.4
  64.4 5.0 all-to-all-start
  69.4 2.4 mul.83
  71.8 2.7 mul.84
  74.8 1.7 convolution_convert_fusion.3
  76.5 8.6 %all-to-all-done = bf16[8,40,2048]{2,1,0:T(8,128)(2,1)} async-done(((bf16[8,40,2048]{2,1,0:T(8,128)(2,1)}), bf16[8,40,2048]{2,1,0:T(8,128)(2,1)}, u32[]{:S(2)}, u32[]{:S(2)}) %all-to-all-start) | async-done | bytes 1310752 | tf_op jit(solution)/shard_map/all_to_all | solution.py:80
  85.1 4.7 all-to-all-start.5
  89.8 28.4 %all-gather.9.cloned.1.call-done = bf16[1,2048,768]{2,1,0:T(8,128)(2,1)} async-done(((bf16[1,64,768]{2,1,0:T(8,128)(2,1)}), bf16[1,2048,768]{2,1,0:T(8,128)(2,1)}) %all-gather.9.cloned.1.call-update) | async-done | bytes 3145744 | tf_op jit(solution)/shard_map/all_gather | solution.py:73
  118.3 3.5 fusion.6
  121.7 84.2 %all-gather.11.cloned.1.call-done = bf16[1,768,2048]{1,2,0:T(8,128)(2,1)} async-done(((bf16[1,768,64]{1,2,0:T(8,128)(2,1)}), bf16[1,768,2048]{1,2,0:T(8,128)(2,1)}) %all-gather.11.cloned.1.call-update) | async-done | bytes 3145744 | tf_op jit(solution)/shard_map/all_gather | solution.py:74
  206.0 3.5 fusion
  209.4 79.6 %all-gather.7.cloned.1.call-done = bf16[1,2048,768]{2,1,0:T(8,128)(2,1)} async-done(((bf16[1,64,768]{2,1,0:T(8,128)(2,1)}), bf16[1,2048,768]{2,1,0:T(8,128)(2,1)}) %all-gather.7.cloned.1.call-update) | async-done | bytes 3145744 | tf_op jit(solution)/shard_map/all_gather | solution.py:72
  289.0 3.7 multiply_convert_fusion.3
  292.8 0.8 copy-done.15
  293.6 4.8 convolution_convert_fusion
  298.6 4.9 convolution_convert_fusion.1
  303.6 4.8 convolution_convert_fusion.2
  308.5 3.3 fusion.4
  311.8 2.3 fusion.15
  314.1 5.8 all-to-all-start.6
  320.0 4.3 fusion.18
  324.2 15.0 %all-to-all-done.6 = bf16[8,40,2048]{2,1,0:T(8,128)(2,1)S(1)} async-done(((bf16[8,40,2048]{2,1,0:T(8,128)(2,1)}), bf16[8,40,2048]{2,1,0:T(8,128)(2,1)S(1)}, u32[]{:S(2)}, u32[]{:S(2)}) %all-to-all-start.6) | async-done | bytes 1310752 | tf_op jit(solution)/shard_map/all_to_all | solution.py:130
  339.2 4.9 all-to-all-start.4
  344.1 2.3 gather_fusion.1
  346.5 15.7 %all-to-all-done.4 = bf16[8,40,2048]{2,1,0:T(8,128)(2,1)S(1)} async-done(((bf16[8,40,2048]{2,1,0:T(8,128)(2,1)}), bf16[8,40,2048]{2,1,0:T(8,128)(2,1)S(1)}, u32[]{:S(2)}, u32[]{:S(2)}) %all-to-all-start.4) | async-done | bytes 1310752 | tf_op jit(solution)/shard_map/all_to_all | solution.py:92
  362.1 1.4 gather_fusion
  363.5 2.9 broadcast_select_fusion
  366.4 2.2 reshape.97
  368.6 2.7 reshape.102
  371.9 0.6 copy.27
  372.5 4.7 reduce.1
  377.2 5.6 multiply_reduce_fusion.1
  382.9 44.3 %reduce-scatter.8.cloned.1.call-done = bf16[768,64]{0,1:T(8,128)(2,1)} async-done(((bf16[768,2048]{0,1:T(8,128)(2,1)}), bf16[768,64]{0,1:T(8,128)(2,1)}) %reduce-scatter.8.cloned.1.call-update) | async-done | bytes 98320 | tf_op jit(solution)/shard_map/reduce_scatter | solution.py:153
  427.2 1.6 bitcast_convert_fusion
  428.8 124.2 %reduce-scatter.6.cloned.1.call-done = bf16[64,768]{1,0:T(8,128)(2,1)} async-done(((bf16[2048,768]{1,0:T(8,128)(2,1)}), bf16[64,768]{1,0:T(8,128)(2,1)}) %reduce-scatter.6.cloned.1.call-update) | async-done | bytes 98320 | tf_op jit(solution)/shard_map/reduce_scatter | solution.py:150
  553.0 1.6 bitcast_convert_fusion.1
  554.6 124.2 %reduce-scatter.4.cloned.1.call-done = bf16[64,768]{1,0:T(8,128)(2,1)} async-done(((bf16[2048,768]{1,0:T(8,128)(2,1)}), bf16[64,768]{1,0:T(8,128)(2,1)}) %reduce-scatter.4.cloned.1.call-update) | async-done | bytes 98320 | tf_op jit(solution)/shard_map/reduce_scatter | solution.py:147
  678.8 1.6 bitcast_convert_fusion.2
  (68 shorter events, 4.7 us)
Async XLA Ops:
  7.2 22.5 %copy-start = (bf16[1,768,2048]{2,1,0:T(8,128)(2,1)S(1)}, bf16[1,768,2048]{2,1,0:T(8,128)(2,1)}, u32[]{:S(2)}) copy-start(bf16[1,768,2048]{2,1,0:T(8,128)(2,1)} %param.17) | copy-start | bytes 9437188
  7.2 9.5 %copy-start.11 = (s32[8]{0:T(128)S(1)}, s32[8]{0:T(128)}, u32[]{:S(2)}) copy-start(s32[8]{0:T(128)} %param.14) | copy-start | bytes 100
  10.5 17.6 %all-to-all-start.2 = ((bf16[8,64,768]{2,1,0:T(8,128)(2,1)}), bf16[8,64,768]{2,1,0:T(8,128)(2,1)}, u32[]{:S(2)}, u32[]{:S(2)}) async-start(bf16[8,64,768]{2,1,0:T(8,128)(2,1)} %get-tuple-element.33), calls=%async_computation.2 | async-start | bytes 1572864 | tf_op jit(solution)/shard_map/all_to_all | solution.py:67
  16.7 101.6 %all-gather.9.cloned.1.call-start = ((), (), s32[]{:S(2)}) async-start(), calls=%async_computation.14 | async-start | bytes 3244032 | tf_op jit(solution)/shard_map/all_gather | solution.py:73
  29.7 176.3 %all-gather.11.cloned.1.call-start = ((), (), s32[]{:S(2)}) async-start(), calls=%async_computation.15 | async-start | bytes 3244032 | tf_op jit(solution)/shard_map/all_gather | solution.py:74
  29.9 16.1 %copy-start.6 = (bf16[8,64,768]{2,1,0:T(8,128)(2,1)S(1)}, bf16[8,64,768]{2,1,0:T(8,128)(2,1)}, u32[]{:S(2)}) copy-start(bf16[8,64,768]{2,1,0:T(8,128)(2,1)} %get-tuple-element.32) | copy-start | bytes 2359300
  30.0 30.5 %copy-start.9 = (s32[128,2]{0,1:T(2,128)S(1)}, s32[128,2]{0,1:T(2,128)}, u32[]{:S(2)}) copy-start(s32[128,2]{0,1:T(2,128)} %param.12) | copy-start | bytes 3076
  30.1 31.5 %copy-start.7 = (bf16[128,2048]{1,0:T(8,128)(2,1)S(1)}, bf16[128,2048]{1,0:T(8,128)(2,1)}, u32[]{:S(2)}) copy-start(bf16[128,2048]{1,0:T(8,128)(2,1)} %param.10) | copy-start | bytes 1572868
  45.9 243.1 %all-gather.7.cloned.1.call-start = ((), (), s32[]{:S(2)}) async-start(), calls=%async_computation.13 | async-start | bytes 3244032 | tf_op jit(solution)/shard_map/all_gather | solution.py:72
  62.8 6.6 copy-start.8
  64.4 20.6 %all-to-all-start = ((bf16[8,40,2048]{2,1,0:T(8,128)(2,1)}), bf16[8,40,2048]{2,1,0:T(8,128)(2,1)}, u32[]{:S(2)}, u32[]{:S(2)}) async-start(bf16[8,40,2048]{2,1,0:T(8,128)(2,1)} %bitcast.3), calls=%async_computation | async-start | bytes 2621440 | tf_op jit(solution)/shard_map/all_to_all | solution.py:80
  71.8 2.7 copy-start.10
  74.5 10.6 %copy-start.2 = (f32[256,2048]{1,0:T(8,128)}, f32[256,2048]{1,0:T(8,128)S(1)}, u32[]{:S(2)}) copy-start(f32[256,2048]{1,0:T(8,128)S(1)} %mul.84) | copy-start | bytes 6291460
  85.1 36.6 %all-to-all-start.5 = ((bf16[8,40,2048]{2,1,0:T(8,128)(2,1)}), bf16[8,40,2048]{2,1,0:T(8,128)(2,1)}, u32[]{:S(2)}, u32[]{:S(2)}) async-start(bf16[8,40,2048]{2,1,0:T(8,128)(2,1)} %bitcast.70), calls=%async_computation.5 | async-start | bytes 2621440 | tf_op jit(solution)/shard_map/all_to_all | solution.py:115
  89.8 337.4 %reduce-scatter.8.cloned.1.call-start = ((), (), s32[]{:S(2)}) async-start(), calls=%async_computation.12 | async-start | bytes 3244032 | tf_op jit(solution)/shard_map/reduce_scatter | solution.py:153
  292.8 0.8 copy-start.15
  292.8 10.8 %copy-start.13 = (bf16[320,768]{1,0:T(8,128)(2,1)}, bf16[320,768]{1,0:T(8,128)(2,1)S(1)}, u32[]{:S(2)}) copy-start(bf16[320,768]{1,0:T(8,128)(2,1)S(1)} %get-tuple-element.27) | copy-start | bytes 1474564
  298.4 254.6 %reduce-scatter.6.cloned.1.call-start = ((), (), s32[]{:S(2)}) async-start(), calls=%async_computation.11 | async-start | bytes 3244032 | tf_op jit(solution)/shard_map/reduce_scatter | solution.py:150
  303.5 375.3 %reduce-scatter.4.cloned.1.call-start = ((), (), s32[]{:S(2)}) async-start(), calls=%async_computation.10 | async-start | bytes 3244032 | tf_op jit(solution)/shard_map/reduce_scatter | solution.py:147
  308.5 3.3 copy-start.12
  308.5 3.3 copy-start.14
  314.1 5.8 copy-start.16
  314.1 25.1 %all-to-all-start.6 = ((bf16[8,40,2048]{2,1,0:T(8,128)(2,1)}), bf16[8,40,2048]{2,1,0:T(8,128)(2,1)S(1)}, u32[]{:S(2)}, u32[]{:S(2)}) async-start(bf16[8,40,2048]{2,1,0:T(8,128)(2,1)} %bitcast.16), calls=%async_computation.6 | async-start | bytes 2621440 | tf_op jit(solution)/shard_map/all_to_all | solution.py:130
  339.2 22.9 %all-to-all-start.4 = ((bf16[8,40,2048]{2,1,0:T(8,128)(2,1)}), bf16[8,40,2048]{2,1,0:T(8,128)(2,1)S(1)}, u32[]{:S(2)}, u32[]{:S(2)}) async-start(bf16[8,40,2048]{2,1,0:T(8,128)(2,1)} %bitcast.71), calls=%async_computation.4 | async-start | bytes 2621440 | tf_op jit(solution)/shard_map/all_to_all | solution.py:92
  363.5 2.9 copy-start.4
  366.4 4.9 copy-start.5
  368.6 2.7 copy-start.3
  372.5 307.9 %copy-start.1 = (bf16[1,768,2048]{2,1,0:T(8,128)(2,1)S(1)}, bf16[1,768,2048]{2,1,0:T(8,128)(2,1)}, u32[]{:S(2)}) copy-start(bf16[1,768,2048]{2,1,0:T(8,128)(2,1)} %param.17) | copy-start | bytes 9437188
Sparse Core Ops, SparseCore 0:
  29.8 88.4 all-gather.8
  121.6 84.3 all-gather.10
  209.3 79.6 all-gather.6
  298.5 128.5 reduce-scatter.7
  431.2 121.7 reduce-scatter.5
  557.0 121.7 reduce-scatter.3
where the time goes:
time: 689 us; the launch traced here: 687 us
  waiting for transfers between devices  533 us (77%)
  matrix products  38.3 us (6%)
  blocking collectives  28.9 us (4%)
  starting transfers between devices  27 us (4%)
  local copies, waits for them, and re-layouts  21.9 us (3%)
  other arithmetic  21.5 us (3%)
  between operations  16.3 us (2%)
    reduce_scatter x1, waiting for transfers between devices, shards(): lax.psum_scatter(partial_gate.astype(jnp.bfloat16), 'dp', scatter_dimensi...  124 us
    reduce_scatter x1, waiting for transfers between devices, shards(): lax.psum_scatter(partial_up.astype(jnp.bfloat16), 'dp', scatter_dimension...  124 us
    all_gather x1, waiting for transfers between devices, shards(): lax.all_gather(mate_shares[2], 'dp', axis=1, tiled=True)  84.2 us
    all_gather x1, waiting for transfers between devices, shards(): lax.all_gather(mate_shares[0], 'dp', axis=0, tiled=True)  79.6 us
    reduce_scatter x1, waiting for transfers between devices, shards(): lax.psum_scatter(partial_down.astype(jnp.bfloat16), 'dp', scatter_dimensi...  44.3 us
    all_to_all x2, blocking collectives, shards(): lax.all_to_all(as_sent(outgoing), 'expert', split_axis=0, concat_axis=0,...  28.9 us
    all_gather x1, waiting for transfers between devices, shards(): lax.all_gather(mate_shares[1], 'dp', axis=0, tiled=True)  28.4 us
    all_to_all x1, waiting for transfers between devices, shards(): lax.all_to_all(expert_out.reshape(groups, capacity, model_width), 'expert...  15.7 us
  transfers between devices with their start and end apart: 11, of which 10 were waited for; matrix products, arithmetic and copies ran while one was open for 10% of the time, Pallas kernels for 0%

commit v1 on v0

--- a/solution.py
+++ b/solution.py
@@ -2,14 +2,6 @@
 import jax.numpy as jnp
 from jax import lax
 from jax.sharding import PartitionSpec as P
-
-
-def as_sent(shard):
-
-    def short(part):
-        return part.astype(jnp.bfloat16) if part.dtype == jnp.float32 else part
-
-    return jax.tree.map(short, shard)
 
 
 def contract_rows(left_mat, right_mat):
@@ -38,41 +30,14 @@
     group_ids = jnp.arange(groups, dtype=jnp.int32)
     my_mate = pick_from(partner, my_group)
     flat_ids = expert_ids.reshape(-1)
-    dest_group = jnp.sum(
-        jnp.where(flat_ids[:, None] == group_ids[None, :], partner[None, :], 0), axis=1
-    )
+    dest_group = flat_ids
     one_hot = (dest_group[:, None] == group_ids[None, :]).astype(jnp.int32)
     earlier = jnp.cumsum(one_hot, axis=0) - one_hot
     slot_index = dest_group * capacity + jnp.sum(earlier * one_hot, axis=1)
     place_mat = (slot_index[None, :] == jnp.arange(buffer_rows, dtype=jnp.int32)[:, None]).astype(
         jnp.bfloat16
     )
-    replicas = lax.axis_size("dp")
-    share_rows = model_width // replicas
-    share_start = lax.axis_index("dp") * share_rows
-    shares = (
-        lax.dynamic_slice_in_dim(w_gate[0], share_start, share_rows, 0),
-        lax.dynamic_slice_in_dim(w_up[0], share_start, share_rows, 0),
-        lax.dynamic_slice_in_dim(w_down[0], share_start, share_rows, 1),
-    )
-    is_mate = (partner == my_group)[:, None, None]
-    outgoing = tuple(
-        (
-            jnp.where(is_mate, own_share[None], jnp.zeros_like(own_share)[None])
-            for own_share in shares
-        )
-    )
-    incoming = jax.tree.map(
-        lambda part, own: part.astype(own.dtype),
-        lax.all_to_all(as_sent(outgoing), "expert", split_axis=0, concat_axis=0, tiled=True),
-        outgoing,
-    )
-    mate_shares = tuple((pick_from(block_piece, my_mate) for block_piece in incoming))
-    gate_mat, up_mat, down_mat = (
-        lax.all_gather(mate_shares[0], "dp", axis=0, tiled=True),
-        lax.all_gather(mate_shares[1], "dp", axis=0, tiled=True),
-        lax.all_gather(mate_shares[2], "dp", axis=1, tiled=True),
-    )
+    gate_mat, up_mat, down_mat = w_gate[0], w_up[0], w_down[0]
     repeated = jnp.repeat(tokens, top_count, axis=0)
     outgoing_rows = jnp.dot(place_mat, repeated, preferred_element_type=jnp.float32).astype(
         jnp.bfloat16
@@ -143,18 +108,20 @@
     partial_gate = contract_rows(expert_in, gate_grad_pre)
     partial_up = contract_rows(expert_in, up_grad_pre)
     partial_down = contract_rows(hidden, grads_in)
-    sum_gate, sum_up, sum_down = (
-        lax.psum_scatter(
-            partial_gate.astype(jnp.bfloat16), "dp", scatter_dimension=0, tiled=True
-        ).astype(jnp.float32),
-        lax.psum_scatter(
-            partial_up.astype(jnp.bfloat16), "dp", scatter_dimension=0, tiled=True
-        ).astype(jnp.float32),
-        lax.psum_scatter(
-            partial_down.astype(jnp.bfloat16), "dp", scatter_dimension=1, tiled=True
-        ).astype(jnp.float32),
+    share_gate = lax.psum_scatter(
+        partial_gate.astype(jnp.bfloat16), "dp", scatter_dimension=0, tiled=True
     )
-    return (mixed_out, token_grad, gate_grad, sum_gate[None], sum_up[None], sum_down[None])
+    share_up = lax.psum_scatter(
+        partial_up.astype(jnp.bfloat16), "dp", scatter_dimension=0, tiled=True
+    )
+    share_down = lax.psum_scatter(
+        partial_down.astype(jnp.bfloat16), "dp", scatter_dimension=1, tiled=True
+    )
+    sums = tuple(
+        pick_from(lax.all_gather(share, "expert", axis=0), my_mate).astype(jnp.float32)
+        for share in (share_gate, share_up, share_down)
+    )
+    return (mixed_out, token_grad, gate_grad, sums[0][None], sums[1][None], sums[2][None])
 
 
 def solution(mesh):

time: 689 us -> 497 us (0.72)
  waiting for transfers between devices: 533 us -> 273 us
  blocking collectives: 28.9 us -> 89.5 us
  local copies, waits for them, and re-layouts: 21.9 us -> 31.9 us
    all_gather x3 -> x0, waiting for transfers between devices: 192 us -> none  [the longest x1 84.2 us: shards(): lax.all_gather(mate_shares[2], 'dp', axis=1, tiled=True)]
    all_gather x0 -> x3, blocking collectives: none -> 89.5 us  [shards(): lax.all_gather(share, 'expert', axis=0)]
    reduce_scatter x1, waiting for transfers between devices: 124 us -> 94.9 us  [shards(): lax.psum_scatter(partial_up.astype(jnp.bfloat16), 'dp', scatter_dimension...]
    all_to_all x2 -> x0, blocking collectives: 28.9 us -> none  [shards(): lax.all_to_all(as_sent(outgoing), 'expert', split_axis=0, concat_axis=0,...]
    reduce_scatter x1, waiting for transfers between devices: 124 us -> 95.9 us  [shards(): lax.psum_scatter(partial_gate.astype(jnp.bfloat16), 'dp', scatter_dimensi...]
    all_to_all x1, waiting for transfers between devices: 0.01 us -> 12.2 us  [shards(): lax.all_to_all(outgoing_grads.reshape(groups, capacity, model_width), 'ex...]
    all_to_all x1, waiting for transfers between devices: 15 us -> 5.97 us  [shards(): lax.all_to_all(row_grad.reshape(groups, capacity, model_width), 'expert',...]
    all_to_all x1 -> x0, waiting for transfers between devices: 8.86 us -> none  [shards(): lax.all_to_all(as_sent(outgoing), 'expert', split_axis=0, concat_axis=0,...]
  transfers between devices with their start and end apart: 11 -> 7, of which waited for: 10 -> 7; matrix products, arithmetic and copies ran while one was open for 10% -> 14% of each run, Pallas kernels for 0% -> 0%
where the time goes in v1:
time: 497 us; the launch traced here: 496 us
  waiting for transfers between devices  273 us (55%)
  blocking collectives  89.5 us (18%)
  matrix products  42.6 us (9%)
  local copies, waits for them, and re-layouts  31.9 us (6%)
  starting transfers between devices  24 us (5%)
  other arithmetic  18.8 us (4%)
  between operations  15.8 us (3%)
    reduce_scatter x1, waiting for transfers between devices, shards(): lax.psum_scatter(partial_gate.astype(jnp.bfloat16), 'dp', scatter_dimensi...  95.9 us
    reduce_scatter x1, waiting for transfers between devices, shards(): lax.psum_scatter(partial_up.astype(jnp.bfloat16), 'dp', scatter_dimension...  94.9 us
    all_gather x3, blocking collectives, shards(): lax.all_gather(share, 'expert', axis=0)  89.5 us
    reduce_scatter x1, waiting for transfers between devices, shards(): lax.psum_scatter(partial_down.astype(jnp.bfloat16), 'dp', scatter_dimensi...  47.1 us
    dot_general x3, matrix products, contract_rows(): lax.dot_general(left_mat, right_mat, (((0,), (0,)), ((), ())), preferred_...  14.8 us
    all_to_all x1, waiting for transfers between devices, shards(): lax.all_to_all(outgoing_grads.reshape(groups, capacity, model_width), 'ex...  12.2 us
    all_to_all x1, waiting for transfers between devices, shards(): lax.all_to_all(expert_out.reshape(groups, capacity, model_width), 'expert...  10.8 us
  transfers between devices with their start and end apart: 7, of which 7 were waited for; matrix products, arithmetic and copies ran while one was open for 14% of the time, Pallas kernels for 0%

profile of v1, /device:TPU:8, one launch (start us, length us, event | category | flops | bytes accessed | tf_op | source)
XLA Modules:
  0.0 495.9 jit_solution(16231095115802935109)
XLA Ops:
  7.2 0.9 copy.17
  8.4 0.6 reduce-window.6
  9.0 0.2 slice_reduce_fusion
  9.4 2.7 broadcast_in_dim.11
  12.0 2.3 reshape.90
  14.3 2.8 convolution_convert_fusion.4
  17.1 6.3 %all-to-all-start = ((bf16[8,40,2048]{2,1,0:T(8,128)(2,1)}), bf16[8,40,2048]{2,1,0:T(8,128)(2,1)}, u32[]{:S(2)}, u32[]{:S(2)}) async-start(bf16[8,40,2048]{2,1,0:T(8,128)(2,1)} %bitcast.60), calls=%async_computation | async-start | bytes 2621440 | tf_op jit(solution)/shard_map/all_to_all | solution.py:45
  23.7 3.4 mul.79
  27.1 3.7 mul.80
  30.7 3.3 convolution_convert_fusion.3
  34.0 6.4 %all-to-all-done = bf16[8,40,2048]{2,1,0:T(8,128)(2,1)} async-done(((bf16[8,40,2048]{2,1,0:T(8,128)(2,1)}), bf16[8,40,2048]{2,1,0:T(8,128)(2,1)}, u32[]{:S(2)}, u32[]{:S(2)}) %all-to-all-start) | async-done | bytes 1310752 | tf_op jit(solution)/shard_map/all_to_all | solution.py:45
  40.4 6.0 %all-to-all-start.2 = ((bf16[8,40,2048]{2,1,0:T(8,128)(2,1)}), bf16[8,40,2048]{2,1,0:T(8,128)(2,1)}, u32[]{:S(2)}, u32[]{:S(2)}) async-start(bf16[8,40,2048]{2,1,0:T(8,128)(2,1)} %bitcast.59), calls=%async_computation.2 | async-start | bytes 2621440 | tf_op jit(solution)/shard_map/all_to_all | solution.py:80
  46.4 4.4 fusion.6
  50.8 12.2 %all-to-all-done.2 = bf16[8,40,2048]{2,1,0:T(8,128)(2,1)} async-done(((bf16[8,40,2048]{2,1,0:T(8,128)(2,1)}), bf16[8,40,2048]{2,1,0:T(8,128)(2,1)}, u32[]{:S(2)}, u32[]{:S(2)}) %all-to-all-start.2) | async-done | bytes 1310752 | tf_op jit(solution)/shard_map/all_to_all | solution.py:80
  63.0 3.6 fusion
  66.7 3.8 multiply_convert_fusion.3
  70.4 0.8 copy-done.5
  71.3 4.8 convolution_convert_fusion
  76.2 5.0 %convolution_convert_fusion.2 = bf16[2048,768]{1,0:T(8,128)(2,1)} fusion(bf16[320,2048]{1,0:T(8,128)(2,1)} %bitcast.3, bf16[320,768]{1,0:T(8,128)(2,1)} %get-tuple-element.15), kind=kOutput, calls=%fused_computation.4 | convolution fusion | flops 1008205824 | bytes 4947968 | tf_op jit(solution)/shard_map/dot_general | solution.py:8
  81.2 0.2 reduce-scatter.6.cloned.1.call-start
  81.4 5.0 %convolution_convert_fusion.1 = bf16[2048,768]{1,0:T(8,128)(2,1)} fusion(bf16[320,2048]{1,0:T(8,128)(2,1)} %bitcast.3, bf16[320,768]{1,0:T(8,128)(2,1)} %get-tuple-element.17), kind=kOutput, calls=%fused_computation.3 | convolution fusion | flops 1008205824 | bytes 4947968 | tf_op jit(solution)/shard_map/dot_general | solution.py:8
  86.4 4.4 fusion.18
  90.7 5.8 %all-to-all-start.1 = ((bf16[8,40,2048]{2,1,0:T(8,128)(2,1)}), bf16[8,40,2048]{2,1,0:T(8,128)(2,1)}, u32[]{:S(2)}, u32[]{:S(2)}) async-start(bf16[8,40,2048]{2,1,0:T(8,128)(2,1)} %bitcast.63), calls=%async_computation.1 | async-start | bytes 2621440 | tf_op jit(solution)/shard_map/all_to_all | solution.py:57
  96.5 3.4 fusion.4
  99.9 2.3 fusion.15
  102.2 10.8 %all-to-all-done.1 = bf16[8,40,2048]{2,1,0:T(8,128)(2,1)} async-done(((bf16[8,40,2048]{2,1,0:T(8,128)(2,1)}), bf16[8,40,2048]{2,1,0:T(8,128)(2,1)}, u32[]{:S(2)}, u32[]{:S(2)}) %all-to-all-start.1) | async-done | bytes 1310752 | tf_op jit(solution)/shard_map/all_to_all | solution.py:57
  113.0 5.7 %all-to-all-start.3 = ((bf16[8,40,2048]{2,1,0:T(8,128)(2,1)}), bf16[8,40,2048]{2,1,0:T(8,128)(2,1)}, u32[]{:S(2)}, u32[]{:S(2)}) async-start(bf16[8,40,2048]{2,1,0:T(8,128)(2,1)} %bitcast.62), calls=%async_computation.3 | async-start | bytes 2621440 | tf_op jit(solution)/shard_map/all_to_all | solution.py:95
  118.7 0.6 dynamic_slice.15
  121.2 4.9 gather_fusion
  126.1 2.3 multiply_reduce_fusion
  128.5 0.6 copy.21
  129.2 6.0 %all-to-all-done.3 = bf16[8,40,2048]{2,1,0:T(8,128)(2,1)} async-done(((bf16[8,40,2048]{2,1,0:T(8,128)(2,1)}), bf16[8,40,2048]{2,1,0:T(8,128)(2,1)}, u32[]{:S(2)}, u32[]{:S(2)}) %all-to-all-start.3) | async-done | bytes 1310752 | tf_op jit(solution)/shard_map/all_to_all | solution.py:95
  135.1 4.8 gather_fusion.1
  140.0 3.5 broadcast_select_fusion
  143.5 2.5 reshape.100
  146.0 3.5 reshape.95
  149.5 4.6 reduce.1
  154.0 5.6 %multiply_reduce_fusion.1 = bf16[128,2048]{1,0:T(8,128)(2,1)} fusion(f32[128,2,2048]{2,1,0:T(2,128)} %reshape.95, f32[128,2]{1,0:T(8,128)S(1)} %copy.16), kind=kLoop, calls=%fused_computation.24 | loop fusion | flops 786432 | bytes 2622464 | tf_op jit(solution)/shard_map/reduce_sum | solution.py:69
  159.6 47.1 %reduce-scatter.8.cloned.1.call-done = bf16[768,64]{0,1:T(8,128)(2,1)} async-done(((bf16[768,2048]{0,1:T(8,128)(2,1)}), bf16[768,64]{0,1:T(8,128)(2,1)}) %reduce-scatter.8.cloned.1.call-update) | async-done | bytes 98320 | tf_op jit(solution)/shard_map/reduce_scatter | solution.py:117
  206.7 29.9 %all-gather.2 = bf16[6144,64]{0,1:T(8,128)(2,1)S(1)} all-gather(bf16[768,64]{0,1:T(8,128)(2,1)} %reduce-scatter.8.cloned.1.call-done), channel_id=4, replica_groups=mesh['dp'=32,'expert'=8] {'expert'}, dimensions={0}, use_global_device_ids=true | all-gather | bytes 884736 | tf_op jit(solution)/shard_map/all_gather | solution.py:121
  236.7 0.2 constant_dynamic-slice_fusion
  236.9 95.9 %reduce-scatter.4.cloned.1.call-done = bf16[64,768]{1,0:T(8,128)(2,1)} async-done(((bf16[2048,768]{1,0:T(8,128)(2,1)}), bf16[64,768]{1,0:T(8,128)(2,1)}) %reduce-scatter.4.cloned.1.call-update) | async-done | bytes 98320 | tf_op jit(solution)/shard_map/reduce_scatter | solution.py:111
  332.8 29.8 %all-gather = bf16[512,768]{1,0:T(8,128)(2,1)S(1)} all-gather(bf16[64,768]{1,0:T(8,128)(2,1)} %reduce-scatter.4.cloned.1.call-done), channel_id=2, replica_groups=mesh['dp'=32,'expert'=8] {'expert'}, dimensions={0}, use_global_device_ids=true | all-gather | bytes 884736 | tf_op jit(solution)/shard_map/all_gather | solution.py:121
  362.6 0.7 dynamic-slice_convert_fusion.1
  363.3 0.7 copy_convert_fusion
  364.0 94.9 %reduce-scatter.6.cloned.1.call-done = bf16[64,768]{1,0:T(8,128)(2,1)} async-done(((bf16[2048,768]{1,0:T(8,128)(2,1)}), bf16[64,768]{1,0:T(8,128)(2,1)}) %reduce-scatter.6.cloned.1.call-update) | async-done | bytes 98320 | tf_op jit(solution)/shard_map/reduce_scatter | solution.py:114
  458.9 29.8 %all-gather.1 = bf16[512,768]{1,0:T(8,128)(2,1)S(1)} all-gather(bf16[64,768]{1,0:T(8,128)(2,1)} %reduce-scatter.6.cloned.1.call-done), channel_id=3, replica_groups=mesh['dp'=32,'expert'=8] {'expert'}, dimensions={0}, use_global_device_ids=true | all-gather | bytes 884736 | tf_op jit(solution)/shard_map/all_gather | solution.py:121
  488.7 0.7 dynamic-slice_convert_fusion
  (29 shorter events, 1.1 us)
Async XLA Ops:
  7.2 59.5 %copy-start = (bf16[1,2048,768]{2,1,0:T(8,128)(2,1)S(1)}, bf16[1,2048,768]{2,1,0:T(8,128)(2,1)}, u32[]{:S(2)}) copy-start(bf16[1,2048,768]{2,1,0:T(8,128)(2,1)} %param.15) | copy-start | bytes 9437188
  14.3 9.1 %copy-start.1 = (f32[128,2]{0,1:T(2,128)S(1)}, f32[128,2]{0,1:T(2,128)}, u32[]{:S(2)}) copy-start(f32[128,2]{0,1:T(2,128)} %param.13) | copy-start | bytes 3076
  17.1 23.3 %all-to-all-start = ((bf16[8,40,2048]{2,1,0:T(8,128)(2,1)}), bf16[8,40,2048]{2,1,0:T(8,128)(2,1)}, u32[]{:S(2)}, u32[]{:S(2)}) async-start(bf16[8,40,2048]{2,1,0:T(8,128)(2,1)} %bitcast.60), calls=%async_computation | async-start | bytes 2621440 | tf_op jit(solution)/shard_map/all_to_all | solution.py:45
  40.4 22.7 %all-to-all-start.2 = ((bf16[8,40,2048]{2,1,0:T(8,128)(2,1)}), bf16[8,40,2048]{2,1,0:T(8,128)(2,1)}, u32[]{:S(2)}, u32[]{:S(2)}) async-start(bf16[8,40,2048]{2,1,0:T(8,128)(2,1)} %bitcast.59), calls=%async_computation.2 | async-start | bytes 2621440 | tf_op jit(solution)/shard_map/all_to_all | solution.py:80
  46.4 160.3 %reduce-scatter.8.cloned.1.call-start = ((), (), s32[]{:S(2)}) async-start(), calls=%async_computation.9 | async-start | bytes 3244032 | tf_op jit(solution)/shard_map/reduce_scatter | solution.py:117
  63.0 3.6 copy-start.3
  70.4 0.8 copy-start.5
  76.1 256.7 %reduce-scatter.4.cloned.1.call-start = ((), (), s32[]{:S(2)}) async-start(), calls=%async_computation.7 | async-start | bytes 3244032 | tf_op jit(solution)/shard_map/reduce_scatter | solution.py:111
  81.2 377.7 %reduce-scatter.6.cloned.1.call-start = ((), (), s32[]{:S(2)}) async-start(), calls=%async_computation.8 | async-start | bytes 3244032 | tf_op jit(solution)/shard_map/reduce_scatter | solution.py:114
  90.7 22.3 %all-to-all-start.1 = ((bf16[8,40,2048]{2,1,0:T(8,128)(2,1)}), bf16[8,40,2048]{2,1,0:T(8,128)(2,1)}, u32[]{:S(2)}, u32[]{:S(2)}) async-start(bf16[8,40,2048]{2,1,0:T(8,128)(2,1)} %bitcast.63), calls=%async_computation.1 | async-start | bytes 2621440 | tf_op jit(solution)/shard_map/all_to_all | solution.py:57
  96.5 3.4 copy-start.4
  102.2 16.5 %copy-start.2 = (s32[8]{0:T(128)S(1)}, s32[8]{0:T(128)}, u32[]{:S(2)}) copy-start(s32[8]{0:T(128)} %param.14) | copy-start | bytes 100
  113.0 22.1 %all-to-all-start.3 = ((bf16[8,40,2048]{2,1,0:T(8,128)(2,1)}), bf16[8,40,2048]{2,1,0:T(8,128)(2,1)}, u32[]{:S(2)}, u32[]{:S(2)}) async-start(bf16[8,40,2048]{2,1,0:T(8,128)(2,1)} %bitcast.62), calls=%async_computation.3 | async-start | bytes 2621440 | tf_op jit(solution)/shard_map/all_to_all | solution.py:95
Sparse Core Ops, SparseCore 0:
  76.2 130.4 reduce-scatter.7
  210.9 121.8 reduce-scatter.3
  337.0 121.8 reduce-scatter.5

commit v2 on v1

--- a/solution.py
+++ b/solution.py
@@ -1,23 +1,191 @@
+import functools
+
 import jax
 import jax.numpy as jnp
 from jax import lax
+from jax.experimental import pallas as pl
+from jax.experimental.pallas import tpu as pltpu
 from jax.sharding import PartitionSpec as P
 
-
-def contract_rows(left_mat, right_mat):
-    return lax.dot_general(
-        left_mat, right_mat, (((0,), (0,)), ((), ())), preferred_element_type=jnp.float32
-    )
+MESH = pl.DeviceIdType.MESH
+RING = 8
+STEPS = RING - 1
+ORDER_UP = (0, 2, 4, 6, 5, 3, 1, 7)
+ORDER_DOWN = (1, 3, 5, 6, 4, 2, 0, 7)
+
+
+def remote(src, dst, send_sem, recv_sem, dp, ex):
+    return pltpu.make_async_remote_copy(
+        src_ref=src,
+        dst_ref=dst,
+        send_sem=send_sem,
+        recv_sem=recv_sem,
+        device_id=(dp, ex),
+        device_id_type=MESH,
+    )
+
+
+def reduce_kernel(
+    partner_ref, x_ref, g_ref, gate_ref, up_ref, hid_ref,
+    out_gate, out_up, out_down,
+    part, pair_in, ring_out, ring_in, kept, cross_out, cross_in, share, gathered,
+    pair_s, pair_r, ring_s, ring_r, cross_s, cross_r, ex_s, ex_r,
+):
+    dp = lax.axis_index("dp")
+    ex = lax.axis_index("expert")
+    z, half, core = dp // 4, (dp // 2) % 2, dp % 2
+    ex_x, ex_y = ex // 2, ex % 2
+
+    def at(zz, hh, cc):
+        return zz * 4 + hh * 2 + cc
+
+    mate = at(z, half, 1 - core)
+    after = at((z + 1) % RING, half, core)
+    before = at((z + RING - 1) % RING, half, core)
+    across = at(z, 1 - half, core)
+    offsets = [(dx, dy) for dx in range(4) for dy in range(2) if (dx, dy) != (0, 0)]
+
+    def peer(dx, dy):
+        return ((ex_x + dx) % 4) * 2 + (ex_y + dy) % 2
+
+    def source(dx, dy):
+        return ((ex_x + 4 - dx) % 4) * 2 + (ex_y + 2 - dy) % 2
+
+    barrier = pltpu.get_barrier_semaphore()
+    for other in (mate, after, before, across):
+        pl.semaphore_signal(barrier, inc=1, device_id=(other, ex), device_id_type=MESH)
+    for dx, dy in offsets:
+        pl.semaphore_signal(barrier, inc=1, device_id=(dp, peer(dx, dy)), device_id_type=MESH)
+    pl.semaphore_wait(barrier, 4 + len(offsets))
+
+    lefts = (x_ref, x_ref, g_ref)
+    rights = (gate_ref, up_ref, hid_ref)
+    outs = (out_gate, out_up, out_down)
+
+    def chunk_of(k):
+        shift = (RING - 1 - k // 2) if k % 2 == 0 else (k // 2 + 1) % 4
+        return (z + shift) % RING
+
+    def pair_copy(k, m):
+        return remote(
+            part.at[k, m, 1 - core], pair_in.at[k, m],
+            pair_s.at[k, m], pair_r.at[k, m], mate, ex,
+        )
+
+    def produce(k):
+        start = pl.multiple_of(chunk_of(k) * 256, 256)
+        for m in range(3):
+            block = lax.dot_general(
+                lefts[m][:, pl.ds(start, 256)], rights[m][...],
+                (((0,), (0,)), ((), ())), preferred_element_type=jnp.float32,
+            ).astype(jnp.bfloat16)
+            for hh in range(2):
+                for cc in range(2):
+                    row = (hh * 2 + cc) * 64
+                    part[k, m, cc, hh] = block[row:row + 64]
+            pair_copy(k, m).start()
+
+    paired = set()
+
+    def local_sum(k, m, way):
+        if (k, m) not in paired:
+            paired.add((k, m))
+            pair_copy(k, m).wait()
+        return part[k, m, core, way].astype(jnp.float32) + pair_in[k, m, way].astype(jnp.float32)
+
+    def ring_copy(m, way, s):
+        return remote(
+            ring_out.at[m, way, s], ring_in.at[m, way, s],
+            ring_s.at[m, way, s], ring_r.at[m, way, s],
+            after if way == 0 else before, ex,
+        )
+
+    def ring(s, m):
+        for way, order in enumerate((ORDER_UP, ORDER_DOWN)):
+            value = local_sum(order[s], m, way)
+            if s > 0:
+                ring_copy(m, way, s - 1).wait()
+                value = value + ring_in[m, way, s - 1].astype(jnp.float32)
+            if s < STEPS:
+                ring_out[m, way, s] = value.astype(jnp.bfloat16)
+                ring_copy(m, way, s).start()
+            else:
+                kept[m, way] = value
+                cross_out[m, way] = value.astype(jnp.bfloat16)
+
+    def cross_copy(m):
+        return remote(
+            cross_out.at[m, 1 - half], cross_in.at[m],
+            cross_s.at[m], cross_r.at[m], across, ex,
+        )
+
+    def share_copy(m, i):
+        dx, dy = offsets[i]
+        return remote(
+            share.at[m], gathered.at[m, ex],
+            ex_s.at[m, i], ex_r.at[m, i], dp, peer(dx, dy),
+        )
+
+    produce(0)
+    produce(1)
+    for s in range(STEPS + 1):
+        if s < 3:
+            produce(2 * s + 2)
+            produce(2 * s + 3)
+        for m in range(3):
+            ring(s, m)
+            if s == STEPS:
+                cross_copy(m).start()
+    for m in range(3):
+        cross_copy(m).wait()
+        total = (kept[m, half] + cross_in[m].astype(jnp.float32)).astype(jnp.bfloat16)
+        share[m] = total
+        gathered[m, ex] = total
+        for i in range(len(offsets)):
+            share_copy(m, i).start()
+    mine = partner_ref[ex]
+    for m in range(3):
+        for i in range(len(offsets)):
+            share_copy(m, i).wait()
+    for m in range(3):
+        outs[m][...] = gathered[m, mine].astype(jnp.float32)
+
+
+def reduce_grads(partner, x, g, gate, up, hid):
+    bf, f32 = jnp.bfloat16, jnp.float32
+    vmem = pl.BlockSpec(memory_space=pltpu.VMEM)
+    dma = pltpu.SemaphoreType.DMA
+    width = gate.shape[1]
+    return pl.pallas_call(
+        reduce_kernel,
+        out_shape=[jax.ShapeDtypeStruct((64, width), f32)] * 3,
+        in_specs=[pl.BlockSpec(memory_space=pltpu.SMEM)] + [vmem] * 5,
+        out_specs=[vmem] * 3,
+        scratch_shapes=[
+            pltpu.VMEM((RING, 3, 2, 2, 64, width), bf),
+            pltpu.VMEM((RING, 3, 2, 64, width), bf),
+            pltpu.VMEM((3, 2, STEPS, 64, width), bf),
+            pltpu.VMEM((3, 2, STEPS, 64, width), bf),
+            pltpu.VMEM((3, 2, 64, width), f32),
+            pltpu.VMEM((3, 2, 64, width), bf),
+            pltpu.VMEM((3, 64, width), bf),
+            pltpu.VMEM((3, 64, width), bf),
+            pltpu.VMEM((3, 8, 64, width), bf),
+            dma((RING, 3)), dma((RING, 3)),
+            dma((3, 2, STEPS)), dma((3, 2, STEPS)),
+            dma((3,)), dma((3,)),
+            dma((3, 7)), dma((3, 7)),
+        ],
+        compiler_params=pltpu.CompilerParams(
+            collective_id=0, has_side_effects=True, vmem_limit_bytes=60 * 1024 * 1024
+        ),
+    )(partner, x, g, gate, up, hid)
 
 
 def contract_cols(left_mat, right_mat):
     return lax.dot_general(
         left_mat, right_mat, (((1,), (1,)), ((), ())), preferred_element_type=jnp.float32
     )
-
-
-def pick_from(stacked, source):
-    return lax.dynamic_index_in_dim(stacked, source, 0, keepdims=False)
 
 
 def shards(tokens, cotangent, expert_ids, gate_weights, partner, w_gate, w_up, w_down):
@@ -28,7 +196,6 @@
     capacity = min(tok_count, 5 * tok_count * top_count // (4 * groups))
     buffer_rows = groups * capacity
     group_ids = jnp.arange(groups, dtype=jnp.int32)
-    my_mate = pick_from(partner, my_group)
     flat_ids = expert_ids.reshape(-1)
     dest_group = flat_ids
     one_hot = (dest_group[:, None] == group_ids[None, :]).astype(jnp.int32)
@@ -105,23 +272,10 @@
         .reshape(tok_count, top_count, model_width)
     )
     token_grad = jnp.sum(grad_rows, axis=1).astype(jnp.bfloat16)
-    partial_gate = contract_rows(expert_in, gate_grad_pre)
-    partial_up = contract_rows(expert_in, up_grad_pre)
-    partial_down = contract_rows(hidden, grads_in)
-    share_gate = lax.psum_scatter(
-        partial_gate.astype(jnp.bfloat16), "dp", scatter_dimension=0, tiled=True
-    )
-    share_up = lax.psum_scatter(
-        partial_up.astype(jnp.bfloat16), "dp", scatter_dimension=0, tiled=True
-    )
-    share_down = lax.psum_scatter(
-        partial_down.astype(jnp.bfloat16), "dp", scatter_dimension=1, tiled=True
-    )
-    sums = tuple(
-        pick_from(lax.all_gather(share, "expert", axis=0), my_mate).astype(jnp.float32)
-        for share in (share_gate, share_up, share_down)
-    )
-    return (mixed_out, token_grad, gate_grad, sums[0][None], sums[1][None], sums[2][None])
+    sum_gate, sum_up, sum_down = reduce_grads(
+        partner, expert_in, grads_in, gate_grad_pre, up_grad_pre, hidden
+    )
+    return (mixed_out, token_grad, gate_grad, sum_gate[None], sum_up[None], sum_down.T[None])
 
 
 def solution(mesh):

time: 497 us -> 229 us (0.46)
  waiting for transfers between devices: 273 us -> 29.4 us
  Pallas kernels: 0 us -> 96.6 us
  blocking collectives: 89.5 us -> 0 us
  matrix products: 42.6 us -> 25.9 us
  between operations: 15.8 us -> 0.75 us
    reduce_scatter x3 -> x0, waiting for transfers between devices: 238 us -> none  [the longest x1 95.9 us: shards(): lax.psum_scatter(partial_gate.astype(jnp.bfloat16), 'dp', scatter_dimensi...]
    pallas_call x0 -> x1, Pallas kernels: none -> 96.6 us  [reduce_grads(): pl.pallas_call(reduce_kernel, out_shape=[jax.ShapeDtypeStruct((64, width)...]
    all_gather x3 -> x0, blocking collectives: 89.5 us -> none  [shards(): lax.all_gather(share, 'expert', axis=0)]
    dot_general x3 -> x0, matrix products: 14.8 us -> none  [contract_rows(): lax.dot_general(left_mat, right_mat, (((0,), (0,)), ((), ())), preferred_...]
    all_to_all x1, waiting for transfers between devices: 5.97 us -> 0.01 us  [shards(): lax.all_to_all(row_grad.reshape(groups, capacity, model_width), 'expert',...]
  transfers between devices with their start and end apart: 7 -> 4, of which waited for: 7 -> 3; matrix products, arithmetic and copies ran while one was open for 14% -> 13% of each run, Pallas kernels for 0% -> 42%
where the time goes in v2:
time: 229 us; the launch traced here: 228 us
  Pallas kernels  96.6 us (42%)
  local copies, waits for them, and re-layouts  34.4 us (15%)
  waiting for transfers between devices  29.4 us (13%)
  matrix products  25.9 us (11%)
  starting transfers between devices  23.8 us (10%)
  other arithmetic  16.7 us (7%)
    pallas_call x1, Pallas kernels, reduce_grads(): pl.pallas_call(reduce_kernel, out_shape=[jax.ShapeDtypeStruct((64, width)...  96.6 us
    all_to_all x1, waiting for transfers between devices, shards(): lax.all_to_all(outgoing_grads.reshape(groups, capacity, model_width), 'ex...  12.2 us
    all_to_all x1, waiting for transfers between devices, shards(): lax.all_to_all(expert_out.reshape(groups, capacity, model_width), 'expert...  10.9 us
    dot_general x3, matrix products, contract_cols(): lax.dot_general(left_mat, right_mat, (((1,), (1,)), ((), ())), preferred_...  9.15 us
    mul x2, local copies, waits for them, and re-layouts, shards(): gate_weights[:, :, None] * cot_float[:, None, :]  7.17 us
    all_to_all x1, starting transfers between devices, shards(): lax.all_to_all(outgoing_rows.reshape(groups, capacity, model_width), 'exp...  6.3 us
    all_to_all x1, waiting for transfers between devices, shards(): lax.all_to_all(outgoing_rows.reshape(groups, capacity, model_width), 'exp...  6.25 us
    all_to_all x1, starting transfers between devices, shards(): lax.all_to_all(outgoing_grads.reshape(groups, capacity, model_width), 'ex...  6.06 us
  transfers between devices with their start and end apart: 4, of which 3 were waited for; matrix products, arithmetic and copies ran while one was open for 13% of the time, Pallas kernels for 42%

profile of v2, /device:TPU:8, one launch (start us, length us, event | category | flops | bytes accessed | tf_op | source)
XLA Modules:
  0.0 227.6 jit_solution(8846332499480119947)
XLA Ops:
  0.6 0.0 copy-start
  0.6 0.9 copy.16
  1.6 0.1 reshape.88
  1.7 0.1 eq.39
  1.9 0.6 reduce-window.6
  2.5 0.2 slice_reduce_fusion
  2.7 0.1 fusion.25
  2.8 2.7 %broadcast_in_dim.28 = bf16[128,2,2048]{2,1,0:T(2,128)(2,1)} broadcast(bf16[128,2048]{1,0:T(8,128)(2,1)} %param.10), dimensions={0,2} | broadcast | bytes 1572864 | tf_op jit(solution)/shard_map/broadcast_in_dim | solution.py:208
  5.5 2.3 reshape.90
  7.8 2.8 %convolution_convert_fusion.1 = bf16[320,2048]{1,0:T(8,128)(2,1)} fusion(bf16[256,2048]{1,0:T(8,128)(2,1)} %reshape.90, s32[256]{0:T(256)S(1)} %get-tuple-element.20), kind=kOutput, calls=%fused_computation.18 | convolution fusion | flops 336281600 | bytes 2360320 | tf_op jit(solution)/shard_map/dot_general | solution.py:209
  10.6 6.3 %all-to-all-start = ((bf16[8,40,2048]{2,1,0:T(8,128)(2,1)}), bf16[8,40,2048]{2,1,0:T(8,128)(2,1)}, u32[]{:S(2)}, u32[]{:S(2)}) async-start(bf16[8,40,2048]{2,1,0:T(8,128)(2,1)} %bitcast.51), calls=%async_computation | async-start | bytes 2621440 | tf_op jit(solution)/shard_map/all_to_all | solution.py:212
  16.9 0.1 copy.15
  17.0 0.1 mul.77
  17.2 3.5 %mul.79 = f32[128,2,2048]{2,1,0:T(2,128)} broadcast(bf16[128,2048]{1,0:T(8,128)(2,1)} %param.11), dimensions={0,2} | broadcast | bytes 2621440 | tf_op jit(solution)/shard_map/mul | solution.py:240
  20.6 3.7 %mul.80 = f32[256,2048]{1,0:T(8,128)} reshape(f32[128,2,2048]{2,1,0:T(2,128)} %mul.79) | data formatting | bytes 4194304 | tf_op jit(solution)/shard_map/mul | solution.py:240
  24.3 3.3 %convolution_convert_fusion = bf16[320,2048]{1,0:T(8,128)(2,1)} fusion(f32[256,2048]{1,0:T(8,128)} %mul.80, f32[256]{0:T(256)S(1)} %mul.77, s32[256]{0:T(256)S(1)} %get-tuple-element.20), kind=kOutput, calls=%fused_computation.17 | convolution fusion | flops 337330176 | bytes 3409920 | tf_op jit(solution)/shard_map/dot_general | solution.py:244
  27.6 6.3 %all-to-all-done = bf16[8,40,2048]{2,1,0:T(8,128)(2,1)} async-done(((bf16[8,40,2048]{2,1,0:T(8,128)(2,1)}), bf16[8,40,2048]{2,1,0:T(8,128)(2,1)}, u32[]{:S(2)}, u32[]{:S(2)}) %all-to-all-start) | async-done | bytes 1310752 | tf_op jit(solution)/shard_map/all_to_all | solution.py:212
  33.9 6.1 %all-to-all-start.2 = ((bf16[8,40,2048]{2,1,0:T(8,128)(2,1)}), bf16[8,40,2048]{2,1,0:T(8,128)(2,1)}, u32[]{:S(2)}, u32[]{:S(2)}) async-start(bf16[8,40,2048]{2,1,0:T(8,128)(2,1)} %bitcast.52), calls=%async_computation.2 | async-start | bytes 2621440 | tf_op jit(solution)/shard_map/all_to_all | solution.py:247
  39.9 4.4 %fusion.6 = f32[320,768]{1,0:T(8,128)} fusion(bf16[320,2048]{1,0:T(8,128)(2,1)} %bitcast.3.x_ref, bf16[1,2048,768]{2,1,0:T(8,128)(2,1)} %param.16), kind=kOutput, calls=%fused_computation.8 | convolution fusion | flops 1006632960 | bytes 5439488 | tf_op jit(solution)/shard_map/dot_general | solution.py:220
  44.4 12.2 %all-to-all-done.2 = bf16[8,40,2048]{2,1,0:T(8,128)(2,1)} async-done(((bf16[8,40,2048]{2,1,0:T(8,128)(2,1)}), bf16[8,40,2048]{2,1,0:T(8,128)(2,1)}, u32[]{:S(2)}, u32[]{:S(2)}) %all-to-all-start.2) | async-done | bytes 1310752 | tf_op jit(solution)/shard_map/all_to_all | solution.py:247
  56.6 3.6 %fusion = f32[320,768]{1,0:T(8,128)S(1)} fusion(bf16[320,2048]{1,0:T(8,128)(2,1)} %bitcast.10.g_ref, bf16[1,768,2048]{2,1,0:T(8,128)(2,1)} %param.17), kind=kOutput, calls=%fused_computation.2 | convolution fusion | flops 1006632960 | bytes 5439488 | tf_op jit(solution)/shard_map/dot_general | solution.py:186
  60.2 0.0 copy-done
  60.2 0.0 copy-done.6
  60.2 0.0 copy-start.5
  60.2 3.9 %multiply_convert_fusion.3 = (bf16[320,768]{1,0:T(8,128)(2,1)}, bf16[320,768]{1,0:T(8,128)(2,1)S(1)}, bf16[320,768]{1,0:T(8,128)(2,1)}) fusion(f32[320,768]{1,0:T(8,128)S(1)} %fusion, f32[320,768]{1,0:T(8,128)S(1)} %copy-done.6, bf16[320,2048]{1,0:T(8,128)(2,1)} %bitcast.3.x_ref, bf16[1,2048,768]{2,1,0:T(8,128)(2,1)S(1)} %copy-done), kind=kOutput, calls=%fused_computation.26 | convolution fusion | flops 1010565120 | bytes 7897088 | tf_op jit(solution)/shard_map/dot_general | solution.py:219
  64.1 0.0 copy-done.5
  64.1 2.3 %fusion.18 = bf16[320,2048]{1,0:T(8,128)(2,1)} fusion(bf16[320,768]{1,0:T(8,128)(2,1)S(1)} %get-tuple-element.22.hid_ref, bf16[1,768,2048]{2,1,0:T(8,128)(2,1)S(1)} %copy-done.5), kind=kOutput, calls=%fused_computation.16 | convolution fusion | flops 1007288320 | bytes 4947968 | tf_op jit(solution)/shard_map/dot_general | solution.py:223
  66.4 5.8 %all-to-all-start.1 = ((bf16[8,40,2048]{2,1,0:T(8,128)(2,1)}), bf16[8,40,2048]{2,1,0:T(8,128)(2,1)}, u32[]{:S(2)}, u32[]{:S(2)}) async-start(bf16[8,40,2048]{2,1,0:T(8,128)(2,1)} %bitcast.54), calls=%async_computation.1 | async-start | bytes 2621440 | tf_op jit(solution)/shard_map/all_to_all | solution.py:224
  72.2 3.3 %fusion.4 = f32[320,2048]{1,0:T(8,128)S(1)} fusion(bf16[320,768]{1,0:T(8,128)(2,1)} %get-tuple-element.23.up_ref, bf16[1,2048,768]{2,1,0:T(8,128)(2,1)} %param.16), kind=kOutput, calls=%fused_computation.6 | convolution fusion | flops 1006632960 | bytes 6258688 | tf_op jit(solution)/shard_map/dot_general | solution.py:186
  75.5 2.3 fusion.15
  77.8 10.9 %all-to-all-done.1 = bf16[8,40,2048]{2,1,0:T(8,128)(2,1)} async-done(((bf16[8,40,2048]{2,1,0:T(8,128)(2,1)}), bf16[8,40,2048]{2,1,0:T(8,128)(2,1)}, u32[]{:S(2)}, u32[]{:S(2)}) %all-to-all-start.1) | async-done | bytes 1310752 | tf_op jit(solution)/shard_map/all_to_all | solution.py:224
  88.7 5.6 %all-to-all-start.3 = ((bf16[8,40,2048]{2,1,0:T(8,128)(2,1)}), bf16[8,40,2048]{2,1,0:T(8,128)(2,1)}, u32[]{:S(2)}, u32[]{:S(2)}) async-start(bf16[8,40,2048]{2,1,0:T(8,128)(2,1)} %bitcast.53), calls=%async_computation.3 | async-start | bytes 2621440 | tf_op jit(solution)/shard_map/all_to_all | solution.py:262
  94.4 96.6 %shard_map.127 = (f32[64,768]{1,0:T(8,128)}, f32[64,768]{1,0:T(8,128)}, f32[64,768]{1,0:T(8,128)}) custom-call(s32[8]{0:T(128)} %partner_ref.1, bf16[320,2048]{1,0:T(8,128)(2,1)} %bitcast.3.x_ref, bf16[320,2048]{1,0:T(8,128)(2,1)} %bitcast.10.g_ref, bf16[320,768]{1,0:T(8,128)(2,1)} %get-tuple-element.21.gate_ref, bf16[320,768]{1,0:T(8,128)(2,1)} %get-tuple-element.23.up_ref, ...), custom_call_target="tpu_custom_call" | custom-call | tf_op jit(solution)/shard_map/pallas_call | solution.py:159
  191.0 4.8 %gather_fusion = bf16[256,2048]{1,0:T(8,128)(2,1)} fusion(bf16[320,2048]{1,0:T(8,128)(2,1)} %bitcast.8, s32[1024]{0:T(1024)S(1)} %pad_clamp_fusion), kind=kCustom, calls=%fused_computation.clone | custom fusion | bytes 2098176 | tf_op jit(solution)/shard_map/jit(_take)/gather | solution.py:232
  195.8 2.3 %multiply_reduce_fusion = f32[256]{0:T(256)S(1)} fusion(f32[256,2048]{1,0:T(8,128)} %mul.80, bf16[256,2048]{1,0:T(8,128)(2,1)} %gather_fusion, pred[256]{0:T(512)(128)(4,1)S(1)} %get-tuple-element.19), kind=kLoop, calls=%fused_computation.19 | loop fusion | flops 2096896 | bytes 3147008 | tf_op jit(solution)/shard_map/reduce_sum | solution.py:238
  198.1 0.1 reduce_sum.42
  198.3 0.6 copy.19
  198.9 0.0 all-to-all-done.3
  198.9 5.0 %gather_fusion.1 = bf16[256,2048]{1,0:T(8,128)(2,1)} fusion(bf16[320,2048]{1,0:T(8,128)(2,1)} %bitcast.12, s32[1024]{0:T(1024)S(1)} %pad_clamp_fusion), kind=kCustom, calls=%fused_computation.1.clone | custom fusion | bytes 2098176 | tf_op jit(solution)/shard_map/jit(_take)/gather | solution.py:270
  204.0 3.5 %broadcast_select_fusion = (bf16[256,2048]{1,0:T(8,128)(2,1)}, f32[256,2048]{1,0:T(8,128)}) fusion(bf16[256,2048]{1,0:T(8,128)(2,1)} %gather_fusion.1, pred[256]{0:T(512)(128)(4,1)S(1)} %get-tuple-element.19, bf16[256,2048]{1,0:T(8,128)(2,1)} %gather_fusion), kind=kLoop, calls=%fused_computation.24 | loop fusion | flops 1572864 | bytes 5243136 | tf_op jit(solution)/shard_map/jit(_take)/select_n | solution.py:270
  207.4 2.5 %reshape.100 = bf16[128,2,2048]{2,1,0:T(2,128)(2,1)} reshape(bf16[256,2048]{1,0:T(8,128)(2,1)} %get-tuple-element.24) | data formatting | bytes 2097152 | tf_op jit(solution)/shard_map/reshape | solution.py:272
  210.0 3.5 %reshape.95 = f32[128,2,2048]{2,1,0:T(2,128)} reshape(f32[256,2048]{1,0:T(8,128)} %get-tuple-element.25) | data formatting | bytes 4194304 | tf_op jit(solution)/shard_map/reshape | solution.py:234
  213.5 5.6 %multiply_reduce_fusion.1 = bf16[128,2048]{1,0:T(8,128)(2,1)} fusion(f32[128,2,2048]{2,1,0:T(2,128)} %reshape.95, f32[128,2]{1,0:T(8,128)S(1)} %copy.15), kind=kLoop, calls=%fused_computation.21 | loop fusion | flops 786432 | bytes 2622464 | tf_op jit(solution)/shard_map/reduce_sum | solution.py:236
  219.1 4.6 %reduce.1 = bf16[128,2048]{1,0:T(8,128)(2,1)} reduce(bf16[128,2,2048]{2,1,0:T(2,128)(2,1)} %reshape.100, bf16[]{:T(256)} %constant.29), dimensions={1}, to_apply=%region_4.6.clone | reduce | flops 262144 | bytes 1572866 | tf_op jit(solution)/shard_map/reduce_sum | solution.py:274
  223.7 1.6 copy.23
  225.3 1.6 copy.24
  226.9 0.0 copy-done.3
  226.9 0.7 copy.25
  (14 shorter events, 0.1 us)
Async XLA Ops:
  0.6 59.5 %copy-start = (bf16[1,2048,768]{2,1,0:T(8,128)(2,1)S(1)}, bf16[1,2048,768]{2,1,0:T(8,128)(2,1)}, u32[]{:S(2)}) copy-start(bf16[1,2048,768]{2,1,0:T(8,128)(2,1)} %param.15) | copy-start | bytes 9437188
  7.8 9.1 %copy-start.4 = (f32[128,2]{0,1:T(2,128)S(1)}, f32[128,2]{0,1:T(2,128)}, u32[]{:S(2)}) copy-start(f32[128,2]{0,1:T(2,128)} %param.13) | copy-start | bytes 3076
  10.6 23.3 %all-to-all-start = ((bf16[8,40,2048]{2,1,0:T(8,128)(2,1)}), bf16[8,40,2048]{2,1,0:T(8,128)(2,1)}, u32[]{:S(2)}, u32[]{:S(2)}) async-start(bf16[8,40,2048]{2,1,0:T(8,128)(2,1)} %bitcast.51), calls=%async_computation | async-start | bytes 2621440 | tf_op jit(solution)/shard_map/all_to_all | solution.py:212
  33.9 22.7 %all-to-all-start.2 = ((bf16[8,40,2048]{2,1,0:T(8,128)(2,1)}), bf16[8,40,2048]{2,1,0:T(8,128)(2,1)}, u32[]{:S(2)}, u32[]{:S(2)}) async-start(bf16[8,40,2048]{2,1,0:T(8,128)(2,1)} %bitcast.52), calls=%async_computation.2 | async-start | bytes 2621440 | tf_op jit(solution)/shard_map/all_to_all | solution.py:247
  56.6 3.6 %copy-start.6 = (f32[320,768]{1,0:T(8,128)S(1)}, f32[320,768]{1,0:T(8,128)}, u32[]{:S(2)}) copy-start(f32[320,768]{1,0:T(8,128)} %fusion.6) | copy-start | bytes 2949124
  60.2 3.9 %copy-start.5 = (bf16[1,768,2048]{2,1,0:T(8,128)(2,1)S(1)}, bf16[1,768,2048]{2,1,0:T(8,128)(2,1)}, u32[]{:S(2)}) copy-start(bf16[1,768,2048]{2,1,0:T(8,128)(2,1)} %param.17) | copy-start | bytes 9437188
  64.1 2.3 %copy-start.2 = (bf16[320,768]{1,0:T(8,128)(2,1)}, bf16[320,768]{1,0:T(8,128)(2,1)S(1)}, u32[]{:S(2)}) copy-start(bf16[320,768]{1,0:T(8,128)(2,1)S(1)} %get-tuple-element.22.hid_ref) | copy-start | bytes 1474564
  66.4 22.3 %all-to-all-start.1 = ((bf16[8,40,2048]{2,1,0:T(8,128)(2,1)}), bf16[8,40,2048]{2,1,0:T(8,128)(2,1)}, u32[]{:S(2)}, u32[]{:S(2)}) async-start(bf16[8,40,2048]{2,1,0:T(8,128)(2,1)} %bitcast.54), calls=%async_computation.1 | async-start | bytes 2621440 | tf_op jit(solution)/shard_map/all_to_all | solution.py:224
  72.2 3.3 %copy-start.1 = (bf16[320,768]{1,0:T(8,128)(2,1)S(1)}, bf16[320,768]{1,0:T(8,128)(2,1)}, u32[]{:S(2)}) copy-start(bf16[320,768]{1,0:T(8,128)(2,1)} %get-tuple-element.21.gate_ref) | copy-start | bytes 1474564
  88.7 110.2 %all-to-all-start.3 = ((bf16[8,40,2048]{2,1,0:T(8,128)(2,1)}), bf16[8,40,2048]{2,1,0:T(8,128)(2,1)}, u32[]{:S(2)}, u32[]{:S(2)}) async-start(bf16[8,40,2048]{2,1,0:T(8,128)(2,1)} %bitcast.53), calls=%async_computation.3 | async-start | bytes 2621440 | tf_op jit(solution)/shard_map/all_to_all | solution.py:262
  213.5 13.4 %copy-start.3 = (f32[64,768]{1,0:T(8,128)S(1)}, f32[64,768]{1,0:T(8,128)}, u32[]{:S(2)}) copy-start(f32[64,768]{1,0:T(8,128)} %get-tuple-element.12) | copy-start | bytes 589828
